TPU v7x, 128 devices: a whole 4x4x4 slice. The times are simulated.
128 devices in a mesh: cuts: 2 (over x_hi), section: 4 (over y), dp: 16 (over z, x_lo, core).
Axes of the slice: x: 4 (x_hi: 2, x_lo: 2; x = x_hi * 2 + x_lo), y: 4, z: 4, core: 2. Of those that a mesh axis runs over, the one named last changes fastest.
Arguments:
- activations: bfloat16 [2, 4, 4096, 4096], P('cuts', 'section', 'dp'), may hold values from -6 to 6
- upstream_grad: bfloat16 [2, 4, 4096, 4096], P('cuts', 'section', 'dp'), may hold values from -6 to 6
- routes: int32 [2, 4, 4096, 4], P('cuts', 'section', 'dp'), may hold values from 0 to 15, as said below
- router_probs: float32 [2, 4, 4096, 4], P('cuts', 'section', 'dp'), may hold values from 0.2 to 1
- gate_weight: bfloat16 [4, 5376, 4096], P('section', 'dp'), may hold values from -0.09375 to 0.09375
- up_weight: bfloat16 [4, 5376, 4096], P('section', 'dp'), may hold values from -0.09375 to 0.09375
- down_weight: bfloat16 [4, 5376, 4096], P('section', 'dp'), may hold values from -0.078125 to 0.078125
Outputs:
- grad_gate: bfloat16 [4, 5376, 4096], P('section', 'dp')
- grad_up: bfloat16 [4, 5376, 4096], P('section', 'dp')
- grad_down: bfloat16 [4, 5376, 4096], P('section', 'dp')
- prev_grad: bfloat16 [2, 4, 4096, 4096], P('cuts', 'section', 'dp')
Inputs may be any that keep to these rules, and one draw needn't show every extreme that they name: `routes`: each token names 4 different experts. In every aligned block of 256 tokens of one replica and section, from 32 to 64 tokens name expert 0, and in every draw some block has exactly 64.
All inputs are finite; a program needn't handle non-finite values.
Results may differ from a plain program's by a relative error of at most 0.025.
Values may be sent and summed in bfloat16 or wider, within the bound.
No kernel may reach another device: no remote copies, remote signals or barrier semaphores. Data moves between devices by JAX's collectives and lax.ppermute only.
A program may use at most 192 MiB of HBM per device.

v0:
```python
import jax
import jax.numpy as jnp
from jax import lax
from jax.sharding import PartitionSpec as P

CAP = 64


def from_behind(block, axis, distance):
    devices = range(lax.axis_size(axis))
    route = [(i - distance, i) for i in devices if i - distance in devices]
    return lax.ppermute(block, axis, route)


def contract_last(left, right):
    return lax.dot_general(
        left, right, (((1,), (1,)), ((), ())), preferred_element_type=jnp.float32
    )


def contract_first(left, right):
    return lax.dot_general(
        left, right, (((0,), (0,)), ((), ())), preferred_element_type=jnp.float32
    )


def per_device(
    activations, upstream_grad, routes, router_probs, gate_weight, up_weight, down_weight
):
    local_acts = activations[0, 0]
    local_grads = upstream_grad[0, 0]
    expert_hits = routes[0, 0] == 0
    router_weight = jnp.sum(jnp.where(expert_hits, router_probs[0, 0], jnp.float32(0.0)), axis=1)
    is_routed = jnp.any(expert_hits, axis=1)
    row_index = jnp.cumsum(is_routed.astype(jnp.int32)) - 1
    wanted = jnp.arange(CAP, dtype=jnp.int32)
    picker = ((row_index[None, :] == wanted[:, None]) & is_routed[None, :]).astype(jnp.bfloat16)
    scaled = (router_weight[:, None] * local_grads.astype(jnp.float32)).astype(jnp.bfloat16)
    packed_acts = jnp.dot(picker, local_acts, preferred_element_type=jnp.float32).astype(
        jnp.bfloat16
    )
    packed_grads = jnp.dot(picker, scaled, preferred_element_type=jnp.float32).astype(jnp.bfloat16)
    rows_acts, rows_grads = (
        lax.all_gather(packed_acts, "dp", axis=0, tiled=True),
        lax.all_gather(packed_grads, "dp", axis=0, tiled=True),
    )
    gate_local = gate_weight[0]
    up_local = up_weight[0]
    down_local = down_weight[0]
    gate_pre = contract_last(rows_acts, gate_local)
    up_pre = contract_last(rows_acts, up_local)
    sig_gate = jax.nn.sigmoid(gate_pre)
    silu_gate = gate_pre * sig_gate
    hidden = (silu_gate * up_pre).astype(jnp.bfloat16)
    hidden_grad = contract_last(rows_grads, down_local)
    gate_grad = (hidden_grad * up_pre * sig_gate * (1.0 + gate_pre * (1.0 - sig_gate))).astype(
        jnp.bfloat16
    )
    up_grad = (hidden_grad * silu_gate).astype(jnp.bfloat16)
    down_part = contract_first(hidden, rows_grads)
    gate_part = contract_first(gate_grad, rows_acts)
    up_part = contract_first(up_grad, rows_acts)
    gate_total, up_total, down_total = (
        lax.psum(gate_part.astype(jnp.bfloat16), "cuts").astype(jnp.float32),
        lax.psum(up_part.astype(jnp.bfloat16), "cuts").astype(jnp.float32),
        lax.psum(down_part.astype(jnp.bfloat16), "cuts").astype(jnp.float32),
    )
    input_rows = lax.psum_scatter(
        (
            jnp.dot(gate_grad, gate_local, preferred_element_type=jnp.float32)
            + jnp.dot(up_grad, up_local, preferred_element_type=jnp.float32)
        ).astype(jnp.bfloat16),
        "dp",
        scatter_dimension=0,
        tiled=True,
    )
    token_grad = contract_first(picker, input_rows).astype(jnp.bfloat16)
    prev_grad = from_behind(token_grad[None, None], "section", -1)
    grad_gate = gate_total.astype(jnp.bfloat16)[None]
    grad_up = up_total.astype(jnp.bfloat16)[None]
    grad_down = down_total.astype(jnp.bfloat16)[None]
    return (grad_gate, grad_up, grad_down, prev_grad)


def solution(mesh):
    placed = (
        P("cuts", "section", "dp", None),
        P("cuts", "section", "dp", None),
        P("cuts", "section", "dp", None),
        P("cuts", "section", "dp", None),
        P("section", "dp", None),
        P("section", "dp", None),
        P("section", "dp", None),
    )
    return jax.shard_map(
        per_device,
        mesh=mesh,
        in_specs=placed,
        out_specs=(
            P("section", "dp", None),
            P("section", "dp", None),
            P("section", "dp", None),
            P("cuts", "section", "dp", None),
        ),
        check_vma=False,
    )
```

profile of v0, /device:TPU:1, one launch (start us, length us, event | category | flops | bytes accessed | tf_op | source)
XLA Modules:
  0.0 471.8 jit_solution(16867495214857487981)
XLA Ops:
  7.2 0.0 all-gather.5.cloned.1.call-start
  7.2 0.9 select_reduce_fusion
  8.1 0.3 reduce-window.9
  8.4 0.1 slice.7
  8.6 0.1 slice_reduce_fusion
  8.7 0.1 add_bitcast_fusion
  8.7 2.9 convolution_convert_fusion.4
  11.6 0.0 all-gather.3.cloned.1.call-start
  11.7 3.0 convolution_convert_fusion.5
  14.7 0.0 reduce-scatter.2.cloned.1.call-start
  14.8 52.8 %all-gather.5.cloned.1.call-done = bf16[1024,4096]{1,0:T(8,128)(2,1)} async-done(((bf16[64,4096]{1,0:T(8,128)(2,1)}), bf16[1024,4096]{1,0:T(8,128)(2,1)}) %all-gather.5.cloned.1.call-update) | async-done | bytes 8388624 | tf_op jit(solution)/shard_map/all_gather | solution.py:44
  67.6 7.6 %fusion.7 = f32[1024,336]{0,1:T(8,128)} fusion(bf16[1024,4096]{1,0:T(8,128)(2,1)} %all-gather.5.cloned.1.call-done, bf16[1,336,4096]{2,1,0:T(8,128)(2,1)S(1)} %copy-done), kind=kOutput, calls=%fused_computation.15 | convolution fusion | flops 2818572288 | bytes 12517376 | tf_op jit(solution)/shard_map/dot_general | solution.py:16
  75.2 4.1 fusion.10
  79.3 43.7 %all-gather.3.cloned.1.call-done = bf16[1024,4096]{1,0:T(8,128)(2,1)} async-done(((bf16[64,4096]{1,0:T(8,128)(2,1)}), bf16[1024,4096]{1,0:T(8,128)(2,1)}) %all-gather.3.cloned.1.call-update) | async-done | bytes 8388624 | tf_op jit(solution)/shard_map/all_gather | solution.py:45
  123.0 8.3 %multiply_convert_fusion.1 = (bf16[1024,336]{0,1:T(8,128)(2,1)S(1)}, bf16[1024,336]{0,1:T(8,128)(2,1)S(1)}) fusion(f32[1024,336]{0,1:T(8,128)} %fusion.7, f32[1024,336]{0,1:T(8,128)} %fusion.10, bf16[1024,4096]{1,0:T(8,128)(2,1)} %all-gather.3.cloned.1.call-done, bf16[1,336,4096]{2,1,0:T(8,128)(2,1)} %param.13), kind=kOutput, calls=%fused_computation.26 | convolution fusion | flops 2823045120 | bytes 15269888 | tf_op jit(solution)/shard_map/dot_general | solution.py:16
  131.4 8.3 %fusion.5 = f32[1024,4096]{1,0:T(8,128)} fusion(bf16[1024,336]{0,1:T(8,128)(2,1)S(1)} %get-tuple-element.10, bf16[1,336,4096]{2,1,0:T(8,128)(2,1)S(1)} %copy-done), kind=kOutput, calls=%fused_computation.13 | convolution fusion | flops 2818572288 | bytes 20217856 | tf_op jit(solution)/shard_map/dot_general | solution.py:70
  139.7 10.2 %add_convert_fusion = bf16[1024,4096]{1,0:T(8,128)(2,1)} fusion(f32[1024,4096]{1,0:T(8,128)} %fusion.5, bf16[1024,336]{0,1:T(8,128)(2,1)S(1)} %get-tuple-element.9, bf16[1,336,4096]{2,1,0:T(8,128)(2,1)S(1)} %copy-done.5), kind=kOutput, calls=%fused_computation | convolution fusion | flops 2826960896 | bytes 28606464 | tf_op jit(solution)/shard_map/dot_general | solution.py:71
  149.9 0.0 all-reduce.3.cloned.1.call-start
  150.0 7.8 %fusion.1 = bf16[1,336,4096]{2,1,0:T(8,128)(2,1)} fusion(bf16[1024,336]{0,1:T(8,128)(2,1)S(1)} %get-tuple-element.9, bf16[1024,4096]{1,0:T(8,128)(2,1)} %all-gather.5.cloned.1.call-done), kind=kOutput, calls=%fused_computation.6 | convolution fusion | flops 2819948544 | bytes 11829248 | tf_op jit(solution)/shard_map/dot_general | solution.py:22
  157.8 8.2 %fusion = bf16[1,336,4096]{2,1,0:T(8,128)(2,1)} fusion(bf16[1024,336]{0,1:T(8,128)(2,1)S(1)} %copy-done.9, bf16[1024,4096]{1,0:T(8,128)(2,1)} %all-gather.5.cloned.1.call-done), kind=kOutput, calls=%fused_computation.5 | convolution fusion | flops 2819948544 | bytes 11829248 | tf_op jit(solution)/shard_map/dot_general | solution.py:22
  166.1 4.5 fusion.2
  170.6 76.1 %reduce-scatter.2.cloned.1.call-done = bf16[64,4096]{1,0:T(8,128)(2,1)} async-done(((bf16[1024,4096]{1,0:T(8,128)(2,1)}), bf16[64,4096]{1,0:T(8,128)(2,1)}) %reduce-scatter.2.cloned.1.call-update) | async-done | bytes 524304 | tf_op jit(solution)/shard_map/reduce_scatter | solution.py:68
  246.7 1.8 fusion.3
  248.5 1.3 collective-permute-start
  249.8 45.3 %collective-permute-done = bf16[1,1,256,4096]{3,2,1,0:T(8,128)(2,1)S(1)} collective-permute-done((bf16[1,1,256,4096]{3,2,1,0:T(8,128)(2,1)S(1)}, bf16[1,1,256,4096]{3,2,1,0:T(8,128)(2,1)S(1)}, u32[]{:S(2)}, u32[]{:S(2)}) %collective-permute-start) | collective-permute-done | bytes 2097184 | tf_op jit(solution)/shard_map/ppermute | solution.py:12
  295.0 159.8 %all-reduce.3.cloned.1.call-done = (bf16[1,336,4096]{2,1,0:T(8,128)(2,1)}, bf16[1,336,4096]{2,1,0:T(8,128)(2,1)}, bf16[1,336,4096]{2,1,0:T(8,128)(2,1)}) async-done(((bf16[1,336,4096]{2,1,0:T(8,128)(2,1)}, bf16[1,336,4096]{2,1,0:T(8,128)(2,1)}, bf16[1,336,4096]{2,1,0:T(8,128)(2,1)}), (bf16[1,336,4096]{2,1,0:T(8,128)(2,1)}, bf16[1,336,4096]{2,1,0:T(8,128)(2,1)}, ...) | async-done | bytes 8257552 | tf_op jit(solution)/shard_map/psum | solution.py:64
  454.8 3.8 copy.15
  458.6 1.5 copy.16
  460.1 1.2 copy-done.2
  461.4 1.5 copy.17
  462.9 1.0 copy-done.7
  463.9 1.3 copy.18
  (36 shorter events, 0.2 us)
Async XLA Ops:
  7.2 60.4 %copy-start = (bf16[1,336,4096]{2,1,0:T(8,128)(2,1)S(1)}, bf16[1,336,4096]{2,1,0:T(8,128)(2,1)}, u32[]{:S(2)}) copy-start(bf16[1,336,4096]{2,1,0:T(8,128)(2,1)} %param.11) | copy-start | bytes 8257540
  7.2 60.4 %all-gather.5.cloned.1.call-start = ((), (), s32[]{:S(2)}) async-start(), calls=%async_computation.2 | async-start | bytes 8912896 | tf_op jit(solution)/shard_map/all_gather | solution.py:44
  11.6 111.4 %all-gather.3.cloned.1.call-start = ((), (), s32[]{:S(2)}) async-start(), calls=%async_computation.1 | async-start | bytes 8912896 | tf_op jit(solution)/shard_map/all_gather | solution.py:45
  14.7 232.0 %reduce-scatter.2.cloned.1.call-start = ((), (), s32[]{:S(2)}) async-start(), calls=%async_computation.3 | async-start | bytes 8912896 | tf_op jit(solution)/shard_map/reduce_scatter | solution.py:68
  67.6 7.7 %copy-start.4 = (bf16[1,336,4096]{2,1,0:T(8,128)(2,1)S(1)}, bf16[1,336,4096]{2,1,0:T(8,128)(2,1)}, u32[]{:S(2)}) copy-start(bf16[1,336,4096]{2,1,0:T(8,128)(2,1)} %param.12) | copy-start | bytes 8257540
  67.6 7.7 %copy-start.10 = (bf16[1024,4096]{1,0:T(8,128)(2,1)S(1)}, bf16[1024,4096]{1,0:T(8,128)(2,1)}, u32[]{:S(2)}) copy-start(bf16[1024,4096]{1,0:T(8,128)(2,1)} %all-gather.5.cloned.1.call-done) | copy-start | bytes 25165828
  131.4 8.3 %copy-start.8 = (bf16[1024,336]{0,1:T(8,128)(2,1)}, bf16[1024,336]{0,1:T(8,128)(2,1)S(1)}, u32[]{:S(2)}) copy-start(bf16[1024,336]{0,1:T(8,128)(2,1)S(1)} %get-tuple-element.10) | copy-start | bytes 2064388
  131.4 8.3 %copy-start.5 = (bf16[1,336,4096]{2,1,0:T(8,128)(2,1)S(1)}, bf16[1,336,4096]{2,1,0:T(8,128)(2,1)}, u32[]{:S(2)}) copy-start(bf16[1,336,4096]{2,1,0:T(8,128)(2,1)} %param.12) | copy-start | bytes 8257540
  149.9 7.9 %copy-start.9 = (bf16[1024,336]{0,1:T(8,128)(2,1)S(1)}, bf16[1024,336]{0,1:T(8,128)(2,1)}, u32[]{:S(2)}) copy-start(bf16[1024,336]{0,1:T(8,128)(2,1)} %copy-done.8) | copy-start | bytes 2064388
  149.9 304.9 %all-reduce.3.cloned.1.call-start = ((), (), s32[]{:S(2)}) async-start(), calls=%async_computation.4 | async-start | bytes 16515072 | tf_op jit(solution)/shard_map/psum | solution.py:64
  150.0 16.1 %slice-start = ((s8[8388608]{0:T(1024)(128)(4,1)}), s8[4194304]{0:T(1024)(128)(4,1)S(1)}, s32[]{:S(2)}) async-start(s8[8388608]{0:T(1024)(128)(4,1)} %bitcast.47), calls=%async_computation.5 | async-start | bytes 8388608
  157.8 8.3 %slice-start.1 = ((s8[8388608]{0:T(1024)(128)(4,1)}), s8[4194304]{0:T(1024)(128)(4,1)S(1)}, s32[]{:S(2)}) async-start(s8[8388608]{0:T(1024)(128)(4,1)} %bitcast.47), calls=%async_computation.6 | async-start | bytes 8388608
  157.8 8.3 %copy-start.11 = (f32[1024,336]{0,1:T(8,128)S(1)}, f32[1024,336]{0,1:T(8,128)}, u32[]{:S(2)}) copy-start(f32[1024,336]{0,1:T(8,128)} %fusion.7) | copy-start | bytes 4128772
  157.8 8.3 %copy-start.12 = (f32[1024,336]{0,1:T(8,128)S(1)}, f32[1024,336]{0,1:T(8,128)}, u32[]{:S(2)}) copy-start(f32[1024,336]{0,1:T(8,128)} %fusion.10) | copy-start | bytes 4128772
  248.5 46.6 %collective-permute-start = (bf16[1,1,256,4096]{3,2,1,0:T(8,128)(2,1)S(1)}, bf16[1,1,256,4096]{3,2,1,0:T(8,128)(2,1)S(1)}, u32[]{:S(2)}, u32[]{:S(2)}) collective-permute-start(bf16[1,1,256,4096]{3,2,1,0:T(8,128)(2,1)S(1)} %fusion.3), channel_id=1, source_target_pairs={{16,0},{32,16},{48,32},{17,1},{33,17},{49,33},{18,2},{34,18},{50,3... | collective-permute-start | bytes 6291464 | tf_op jit(solution)/shard_map/ppermute | solution.py:12
  295.0 159.8 %copy-start.6 = (bf16[1,1,256,4096]{3,2,1,0:T(8,128)(2,1)}, bf16[1,1,256,4096]{3,2,1,0:T(8,128)(2,1)S(1)}, u32[]{:S(2)}) copy-start(bf16[1,1,256,4096]{3,2,1,0:T(8,128)(2,1)S(1)} %collective-permute-done) | copy-start | bytes 6291460
  454.8 3.8 copy-start.3
  458.6 2.8 copy-start.2
  461.4 2.6 copy-start.7
  461.4 3.9 copy-start.1
Sparse Core Ops, SparseCore 0:
  11.8 55.7 all-gather.4
  69.9 53.1 all-gather.2
  150.0 96.6 reduce-scatter.1
  250.0 204.7 all-reduce.2
where the time goes:
time: 472 us
  waiting for transfers between devices  378 us (80%)
  matrix products  66.8 us (14%)
  between operations  13.9 us (3%)
  local copies, waits for them, and re-layouts  10.7 us (2%)
    psum x1, waiting for transfers between devices, per_device(): lax.psum(gate_part.astype(jnp.bfloat16), 'cuts').astype(jnp.float32)  160 us
    reduce_scatter x1, waiting for transfers between devices, per_device(): lax.psum_scatter((jnp.dot(gate_grad, gate_local, preferred_element_type=j...  76.1 us
    all_gather x1, waiting for transfers between devices, per_device(): lax.all_gather(packed_acts, 'dp', axis=0, tiled=True)  52.8 us
    ppermute x1, waiting for transfers between devices, from_behind(): return lax.ppermute(block, axis, route)  45.3 us
    all_gather x1, waiting for transfers between devices, per_device(): lax.all_gather(packed_grads, 'dp', axis=0, tiled=True)  43.7 us
    dot_general x4, matrix products, contract_first(): lax.dot_general(left, right, (((0,), (0,)), ((), ())), preferred_element_...  22.4 us
    dot_general x3, matrix products, contract_last(): lax.dot_general(left, right, (((1,), (1,)), ((), ())), preferred_element_...  20.1 us
    unnamed x34, local copies, waits for them, and re-layouts  10.5 us
  transfers between devices with their start and end apart: 5, of which 5 were waited for; matrix products, arithmetic and copies ran while one was open for 8% of the time, Pallas kernels for 0%

commit v1 on v0

--- a/solution.py
+++ b/solution.py
@@ -61,7 +61,7 @@
     gate_part = contract_first(gate_grad, rows_acts)
     up_part = contract_first(up_grad, rows_acts)
     gate_total, up_total, down_total = (
-        lax.psum(gate_part.astype(jnp.bfloat16), "cuts").astype(jnp.float32),
+        jnp.sum(lax.all_gather(gate_part.astype(jnp.bfloat16), "cuts"), axis=0).astype(jnp.float32),
         lax.psum(up_part.astype(jnp.bfloat16), "cuts").astype(jnp.float32),
         lax.psum(down_part.astype(jnp.bfloat16), "cuts").astype(jnp.float32),
     )

time: 472 us -> 487 us (1.032)
  other arithmetic: 1.32 us -> 7.47 us
  waiting for transfers between devices: 378 us -> 383 us
    all_gather x0 -> x1, waiting for transfers between devices: none -> 73.7 us  [per_device(): lax.all_gather(gate_part.astype(jnp.bfloat16), 'cuts')]
    ppermute x1, waiting for transfers between devices: 45.3 us -> 0.01 us  [from_behind(): return lax.ppermute(block, axis, route)]
    psum x1, waiting for transfers between devices: 160 us -> 141 us  [per_device(): lax.psum(up_part.astype(jnp.bfloat16), 'cuts').astype(jnp.float32)]
    reduce_sum x0 -> x1, other arithmetic: none -> 6.15 us  [per_device(): jnp.sum(lax.all_gather(gate_part.astype(jnp.bfloat16), 'cuts'), axis=0)]
    unnamed x34 -> x27, local copies, waits for them, and re-layouts: 10.5 us -> 8.74 us
  transfers between devices with their start and end apart: 5 -> 6, of which waited for: 5 -> 5; matrix products, arithmetic and copies ran while one was open for 8% -> 10% of each run, Pallas kernels for 0% -> 0%
where the time goes in v1:
time: 487 us; the launch traced here: 486 us
  waiting for transfers between devices  383 us (79%)
  matrix products  71.3 us (15%)
  between operations  13.9 us (3%)
  local copies, waits for them, and re-layouts  8.94 us (2%)
  other arithmetic  7.47 us (2%)
    psum x1, waiting for transfers between devices, per_device(): lax.psum(up_part.astype(jnp.bfloat16), 'cuts').astype(jnp.float32)  141 us
    all_gather x1, waiting for transfers between devices, per_device(): lax.all_gather(gate_part.astype(jnp.bfloat16), 'cuts')  73.7 us
    reduce_scatter x1, waiting for transfers between devices, per_device(): lax.psum_scatter((jnp.dot(gate_grad, gate_local, preferred_element_type=j...  72 us
    all_gather x1, waiting for transfers between devices, per_device(): lax.all_gather(packed_acts, 'dp', axis=0, tiled=True)  52.8 us
    all_gather x1, waiting for transfers between devices, per_device(): lax.all_gather(packed_grads, 'dp', axis=0, tiled=True)  43.7 us
    dot_general x4, matrix products, contract_first(): lax.dot_general(left, right, (((0,), (0,)), ((), ())), preferred_element_...  26.7 us
    dot_general x3, matrix products, contract_last(): lax.dot_general(left, right, (((1,), (1,)), ((), ())), preferred_element_...  20.1 us
    dot_general x1, matrix products, per_device(): jnp.dot(up_grad, up_local, preferred_element_type=jnp.float32)  10.3 us
  transfers between devices with their start and end apart: 6, of which 5 were waited for; matrix products, arithmetic and copies ran while one was open for 10% of the time, Pallas kernels for 0%

profile of v1, /device:TPU:1, one launch (start us, length us, event | category | flops | bytes accessed | tf_op | source)
XLA Modules:
  0.0 486.4 jit_solution(14040392700092671228)
XLA Ops:
  7.2 0.9 select_reduce_fusion
  8.1 0.3 reduce-window.9
  8.4 0.1 slice.7
  8.6 0.1 slice_reduce_fusion
  8.7 0.1 add_bitcast_fusion
  8.7 2.9 convolution_convert_fusion.4
  11.6 0.0 all-gather.5.cloned.1.call-start
  11.7 3.0 convolution_convert_fusion.5
  14.7 0.0 reduce-scatter.2.cloned.1.call-start
  14.8 52.8 %all-gather.7.cloned.1.call-done = bf16[1024,4096]{1,0:T(8,128)(2,1)} async-done(((bf16[64,4096]{1,0:T(8,128)(2,1)}), bf16[1024,4096]{1,0:T(8,128)(2,1)}) %all-gather.7.cloned.1.call-update) | async-done | bytes 8388624 | tf_op jit(solution)/shard_map/all_gather | solution.py:44
  67.6 7.6 %fusion.6 = f32[1024,336]{0,1:T(8,128)} fusion(bf16[1024,4096]{1,0:T(8,128)(2,1)} %all-gather.7.cloned.1.call-done, bf16[1,336,4096]{2,1,0:T(8,128)(2,1)S(1)} %copy-done), kind=kOutput, calls=%fused_computation.14 | convolution fusion | flops 2818572288 | bytes 12517376 | tf_op jit(solution)/shard_map/dot_general | solution.py:16
  75.2 4.1 fusion.9
  79.3 43.7 %all-gather.5.cloned.1.call-done = bf16[1024,4096]{1,0:T(8,128)(2,1)} async-done(((bf16[64,4096]{1,0:T(8,128)(2,1)}), bf16[1024,4096]{1,0:T(8,128)(2,1)}) %all-gather.5.cloned.1.call-update) | async-done | bytes 8388624 | tf_op jit(solution)/shard_map/all_gather | solution.py:45
  123.0 8.3 %multiply_convert_fusion.1 = (bf16[1024,336]{0,1:T(8,128)(2,1)S(1)}, bf16[1024,336]{0,1:T(8,128)(2,1)S(1)}) fusion(f32[1024,336]{0,1:T(8,128)} %fusion.6, f32[1024,336]{0,1:T(8,128)} %fusion.9, bf16[1024,4096]{1,0:T(8,128)(2,1)} %all-gather.5.cloned.1.call-done, bf16[1,336,4096]{2,1,0:T(8,128)(2,1)} %param.13), kind=kOutput, calls=%fused_computation.25 | convolution fusion | flops 2823045120 | bytes 15269888 | tf_op jit(solution)/shard_map/dot_general | solution.py:16
  131.4 8.4 %fusion.4 = f32[1024,4096]{1,0:T(8,128)} fusion(bf16[1024,336]{0,1:T(8,128)(2,1)S(1)} %get-tuple-element.9, bf16[1,336,4096]{2,1,0:T(8,128)(2,1)S(1)} %copy-done), kind=kOutput, calls=%fused_computation.12 | convolution fusion | flops 2818572288 | bytes 20217856 | tf_op jit(solution)/shard_map/dot_general | solution.py:70
  139.8 10.3 %add_convert_fusion = bf16[1024,4096]{1,0:T(8,128)(2,1)} fusion(f32[1024,4096]{1,0:T(8,128)} %fusion.4, bf16[1024,336]{0,1:T(8,128)(2,1)S(1)} %get-tuple-element.8, bf16[1,336,4096]{2,1,0:T(8,128)(2,1)S(1)} %copy-done.4), kind=kOutput, calls=%fused_computation | convolution fusion | flops 2826960896 | bytes 28606464 | tf_op jit(solution)/shard_map/dot_general | solution.py:71
  150.1 0.0 all-gather.9.cloned.1.call-start
  150.1 1.0 copy-done.8
  151.2 7.7 %convolution_convert_fusion.2 = bf16[336,4096]{1,0:T(8,128)(2,1)} fusion(bf16[1024,336]{0,1:T(8,128)(2,1)S(1)} %copy-done.8, bf16[1024,4096]{1,0:T(8,128)(2,1)} %all-gather.7.cloned.1.call-done), kind=kOutput, calls=%fused_computation.3 | convolution fusion | flops 2819948544 | bytes 11829248 | tf_op jit(solution)/shard_map/dot_general | solution.py:22
  158.9 0.0 all-reduce.3.cloned.1.call-start
  158.9 8.1 %fusion = bf16[1,336,4096]{2,1,0:T(8,128)(2,1)} fusion(bf16[1024,336]{0,1:T(8,128)(2,1)S(1)} %get-tuple-element.8, bf16[1024,4096]{1,0:T(8,128)(2,1)} %all-gather.7.cloned.1.call-done), kind=kOutput, calls=%fused_computation.5 | convolution fusion | flops 2819948544 | bytes 11829248 | tf_op jit(solution)/shard_map/dot_general | solution.py:22
  167.0 7.8 %fusion.1 = bf16[1,336,4096]{2,1,0:T(8,128)(2,1)} fusion(bf16[1024,4096]{1,0:T(8,128)(2,1)} %all-gather.5.cloned.1.call-done, f32[1024,336]{0,1:T(8,128)S(1)} %copy-done.11, f32[1024,336]{0,1:T(8,128)S(1)} %copy-done.10), kind=kOutput, calls=%fused_computation.6 | convolution fusion | flops 2822012928 | bytes 13893632 | tf_op jit(solution)/shard_map/dot_general | solution.py:22
  174.9 72.0 %reduce-scatter.2.cloned.1.call-done = bf16[64,4096]{1,0:T(8,128)(2,1)} async-done(((bf16[1024,4096]{1,0:T(8,128)(2,1)}), bf16[64,4096]{1,0:T(8,128)(2,1)}) %reduce-scatter.2.cloned.1.call-update) | async-done | bytes 524304 | tf_op jit(solution)/shard_map/reduce_scatter | solution.py:68
  246.9 3.1 fusion.2
  250.0 1.3 collective-permute-start
  251.3 73.7 %all-gather.9.cloned.1.call-done = bf16[672,4096]{1,0:T(8,128)(2,1)} async-done(((bf16[336,4096]{1,0:T(8,128)(2,1)}), bf16[672,4096]{1,0:T(8,128)(2,1)}) %all-gather.9.cloned.1.call-update) | async-done | bytes 5505040 | tf_op jit(solution)/shard_map/all_gather | solution.py:64
  325.0 6.1 %reduce_sum.22 = bf16[336,4096]{1,0:T(8,128)(2,1)} reduce(bf16[2,336,4096]{2,1,0:T(8,128)(2,1)} %bitcast.47, bf16[]{:T(256)} %constant.15.clone.1), dimensions={0}, to_apply=%region_4.5 | reduce | flops 1376256 | bytes 8257538 | tf_op jit(solution)/shard_map/reduce_sum | solution.py:64
  331.2 141.0 %all-reduce.3.cloned.1.call-done = (bf16[1,336,4096]{2,1,0:T(8,128)(2,1)}, bf16[1,336,4096]{2,1,0:T(8,128)(2,1)}) async-done(((bf16[1,336,4096]{2,1,0:T(8,128)(2,1)}, bf16[1,336,4096]{2,1,0:T(8,128)(2,1)}), (bf16[1,336,4096]{2,1,0:T(8,128)(2,1)}, bf16[1,336,4096]{2,1,0:T(8,128)(2,1)})) %all-reduce.3.cloned.1.call-update) | async-done | bytes 5505040 | tf_op jit(solution)/shard_map/psum | solution.py:65
  472.2 3.8 copy.14
  476.0 1.5 copy.15
  477.5 1.0 copy-done.6
  478.6 1.3 copy.16
  (32 shorter events, 0.2 us)
Async XLA Ops:
  7.2 60.4 %copy-start = (bf16[1,336,4096]{2,1,0:T(8,128)(2,1)S(1)}, bf16[1,336,4096]{2,1,0:T(8,128)(2,1)}, u32[]{:S(2)}) copy-start(bf16[1,336,4096]{2,1,0:T(8,128)(2,1)} %param.11) | copy-start | bytes 8257540
  7.2 60.4 %all-gather.7.cloned.1.call-start = ((), (), s32[]{:S(2)}) async-start(), calls=%async_computation.2 | async-start | bytes 8912896 | tf_op jit(solution)/shard_map/all_gather | solution.py:44
  11.6 111.4 %all-gather.5.cloned.1.call-start = ((), (), s32[]{:S(2)}) async-start(), calls=%async_computation.1 | async-start | bytes 8912896 | tf_op jit(solution)/shard_map/all_gather | solution.py:45
  14.7 232.2 %reduce-scatter.2.cloned.1.call-start = ((), (), s32[]{:S(2)}) async-start(), calls=%async_computation.3 | async-start | bytes 8912896 | tf_op jit(solution)/shard_map/reduce_scatter | solution.py:68
  67.6 7.7 %copy-start.3 = (bf16[1,336,4096]{2,1,0:T(8,128)(2,1)S(1)}, bf16[1,336,4096]{2,1,0:T(8,128)(2,1)}, u32[]{:S(2)}) copy-start(bf16[1,336,4096]{2,1,0:T(8,128)(2,1)} %param.12) | copy-start | bytes 8257540
  67.6 7.7 %copy-start.9 = (bf16[1024,4096]{1,0:T(8,128)(2,1)S(1)}, bf16[1024,4096]{1,0:T(8,128)(2,1)}, u32[]{:S(2)}) copy-start(bf16[1024,4096]{1,0:T(8,128)(2,1)} %all-gather.7.cloned.1.call-done) | copy-start | bytes 25165828
  131.4 8.4 %copy-start.7 = (bf16[1024,336]{0,1:T(8,128)(2,1)}, bf16[1024,336]{0,1:T(8,128)(2,1)S(1)}, u32[]{:S(2)}) copy-start(bf16[1024,336]{0,1:T(8,128)(2,1)S(1)} %get-tuple-element.9) | copy-start | bytes 2064388
  131.4 8.4 %copy-start.4 = (bf16[1,336,4096]{2,1,0:T(8,128)(2,1)S(1)}, bf16[1,336,4096]{2,1,0:T(8,128)(2,1)}, u32[]{:S(2)}) copy-start(bf16[1,336,4096]{2,1,0:T(8,128)(2,1)} %param.12) | copy-start | bytes 8257540
  150.1 1.1 copy-start.8
  150.1 174.9 %all-gather.9.cloned.1.call-start = ((), (), s32[]{:S(2)}) async-start(), calls=%async_computation.4 | async-start | bytes 8257536 | tf_op jit(solution)/shard_map/all_gather | solution.py:64
  158.8 8.2 %copy-start.10 = (f32[1024,336]{0,1:T(8,128)S(1)}, f32[1024,336]{0,1:T(8,128)}, u32[]{:S(2)}) copy-start(f32[1024,336]{0,1:T(8,128)} %fusion.6) | copy-start | bytes 4128772
  158.9 8.2 %copy-start.11 = (f32[1024,336]{0,1:T(8,128)S(1)}, f32[1024,336]{0,1:T(8,128)}, u32[]{:S(2)}) copy-start(f32[1024,336]{0,1:T(8,128)} %fusion.9) | copy-start | bytes 4128772
  158.9 313.3 %all-reduce.3.cloned.1.call-start = ((), (), s32[]{:S(2)}) async-start(), calls=%async_computation.5 | async-start | bytes 11010048 | tf_op jit(solution)/shard_map/psum | solution.py:65
  250.0 81.2 %collective-permute-start = (bf16[1,1,256,4096]{3,2,1,0:T(8,128)(2,1)}, bf16[1,1,256,4096]{3,2,1,0:T(8,128)(2,1)S(1)}, u32[]{:S(2)}, u32[]{:S(2)}) collective-permute-start(bf16[1,1,256,4096]{3,2,1,0:T(8,128)(2,1)} %fusion.2), channel_id=1, source_target_pairs={{16,0},{32,16},{48,32},{17,1},{33,17},{49,33},{18,2},{34,18},{50,3... | collective-permute-start | bytes 6291464 | tf_op jit(solution)/shard_map/ppermute | solution.py:12
  331.2 141.0 %copy-start.5 = (bf16[1,1,256,4096]{3,2,1,0:T(8,128)(2,1)}, bf16[1,1,256,4096]{3,2,1,0:T(8,128)(2,1)S(1)}, u32[]{:S(2)}) copy-start(bf16[1,1,256,4096]{3,2,1,0:T(8,128)(2,1)S(1)} %collective-permute-done) | copy-start | bytes 6291460
  472.2 3.8 copy-start.2
  476.0 2.6 copy-start.6
  476.0 3.9 copy-start.1
Sparse Core Ops, SparseCore 0:
  11.8 55.7 all-gather.6
  69.9 53.1 all-gather.4
  150.2 96.6 reduce-scatter.1
  249.0 75.9 all-gather.8
  328.1 144.0 all-reduce.2
